TPU v7x, 32 devices: a whole 2x2x4 slice. The times are simulated.
32 devices in a mesh: vel: 16 (over z, y, x), space: 2 (over core).
Axes of the slice: x: 2, y: 2, z: 4, core: 2. Of those that a mesh axis runs over, the one named last changes fastest.
Arguments:
- distribution: float32 [16384, 16, 128], P('vel', 'space'), may hold values from 0 to 11, as said below
- rate_class: int32 [16, 128], P('space'), may hold values from 0 to 7
- boundary_obstacle_indicator: int32 [16, 128], P('space'), may hold values 0 or 1
Outputs:
- field_out: float32 [16384, 16, 128], P('vel', 'space')
- latest_conserved_fields: float32 [5, 16, 128], P(None, 'space')
Inputs may be any that keep to these rules, and one draw needn't show every extreme that they name: `distribution`: every entry positive.
All inputs are finite; a program needn't handle non-finite values. No bound on the sum of `boundary_obstacle_indicator` on one device may be relied on, other than what follows from the above.
Results may differ from a plain program's by a relative error of at most 0.0003.
Values sent between devices are 32-bit elements; how exact they have to be, the bound alone decides.
A program may use at most 64 MiB of HBM per device.

v0:
```python
import jax
import jax.numpy as jnp
from jax import lax
from jax.sharding import PartitionSpec as P

VX = 32
VY = 32
VZ = 16
ITERS = 2
SWEEPS = 4
speed_edge = 5.0
marching_step_length = 0.1
momentum_thermal_ratio = 2.0 / 3.0
shear_power_law_index = 0.81
diffusivity = 1.0


def with_halo(value, sides, width):
    for axis, dim in sides:
        size, length = (lax.axis_size(axis), value.shape[dim])
        up = [(i, (i + 1) % size) for i in range(size)]
        down = [(j, i) for i, j in up]
        last = lax.slice_in_dim(value, length - width, length, axis=dim)
        leading = lax.slice_in_dim(value, 0, width, axis=dim)
        before = lax.ppermute(last, axis, up)
        after = lax.ppermute(leading, axis, down)
        value = jnp.concatenate([before, value, after], axis=dim)
    return value


def velocity_table(index):
    index_x = index % VX
    index_y = index // VX % VY
    index_z = index // (VX * VY)
    discrete_abscissa_xaxis = -speed_edge + (index_x.astype(jnp.float32) + 0.5) * (
        2.0 * speed_edge / VX
    )
    discrete_abscissa_yaxis = -speed_edge + (index_y.astype(jnp.float32) + 0.5) * (
        2.0 * speed_edge / VY
    )
    discrete_abscissa_zaxis = -speed_edge + (index_z.astype(jnp.float32) + 0.5) * (
        2.0 * speed_edge / VZ
    )
    return (discrete_abscissa_xaxis, discrete_abscissa_yaxis, discrete_abscissa_zaxis)


def moment_weights(discrete_abscissa_xaxis, discrete_abscissa_yaxis, discrete_abscissa_zaxis):
    square = (
        discrete_abscissa_xaxis * discrete_abscissa_xaxis
        + discrete_abscissa_yaxis * discrete_abscissa_yaxis
        + discrete_abscissa_zaxis * discrete_abscissa_zaxis
    )
    quadrature = (
        2.0
        * speed_edge
        / VX
        * (2.0 * speed_edge / VY)
        * (2.0 * speed_edge / VZ)
        / (2.0 * jnp.pi) ** 1.5
    )
    rows = [
        jnp.ones_like(discrete_abscissa_xaxis),
        discrete_abscissa_xaxis,
        discrete_abscissa_yaxis,
        discrete_abscissa_zaxis,
        square,
        discrete_abscissa_xaxis * discrete_abscissa_xaxis,
        discrete_abscissa_yaxis * discrete_abscissa_yaxis,
        discrete_abscissa_xaxis * discrete_abscissa_yaxis,
        discrete_abscissa_xaxis * discrete_abscissa_zaxis,
        discrete_abscissa_yaxis * discrete_abscissa_zaxis,
        discrete_abscissa_xaxis * square,
        discrete_abscissa_yaxis * square,
        discrete_abscissa_zaxis * square,
    ]
    return jnp.stack(rows) * quadrature


def conserved(moments):
    return jnp.stack([moments[0], moments[1], moments[2], moments[3], 0.5 * moments[4]])


def heat_flux(moments):
    mass = moments[0]
    flow_x = moments[1] / mass
    flow_y = moments[2] / mass
    flow_z = moments[3] / mass
    p_xx = moments[5]
    p_yy = moments[6]
    p_zz = moments[4] - moments[5] - moments[6]
    p_xy = moments[7]
    p_xz = moments[8]
    p_yz = moments[9]
    flow_sq = flow_x * flow_x + flow_y * flow_y + flow_z * flow_z
    heat_x = 0.5 * (
        moments[10]
        - 2.0 * (flow_x * p_xx + flow_y * p_xy + flow_z * p_xz)
        - flow_x * moments[4]
        + 2.0 * mass * flow_sq * flow_x
    )
    heat_y = 0.5 * (
        moments[11]
        - 2.0 * (flow_x * p_xy + flow_y * p_yy + flow_z * p_yz)
        - flow_y * moments[4]
        + 2.0 * mass * flow_sq * flow_y
    )
    heat_z = 0.5 * (
        moments[12]
        - 2.0 * (flow_x * p_xz + flow_y * p_yz + flow_z * p_zz)
        - flow_z * moments[4]
        + 2.0 * mass * flow_sq * flow_z
    )
    return jnp.stack([heat_x, heat_y, heat_z])


def transport(field, courant_x, courant_y):
    from_left = jnp.roll(field, 1, 2)
    from_right = jnp.roll(field, -1, 2)
    term_y = jnp.where(
        courant_y > 0, courant_y * (field - from_left), courant_y * (from_right - field)
    )
    padded = with_halo(field, (("space", 1),), 1)
    term_x = jnp.where(
        courant_x > 0, courant_x * (field - padded[:, :-2]), courant_x * (padded[:, 2:] - field)
    )
    return field - term_x - term_y


def diffuse(source):
    margin = with_halo(source, (("space", 1),), SWEEPS)
    iterate = margin
    for sweep_index in range(SWEEPS):
        inner = iterate[:, 1:-1]
        beside = iterate[:, :-2] + iterate[:, 2:] + jnp.roll(inner, 1, 2) + jnp.roll(inner, -1, 2)
        margin_edge = sweep_index + 1
        iterate = (
            margin[:, margin_edge : margin.shape[1] - margin_edge] + diffusivity * beside
        ) / (1.0 + 4.0 * diffusivity)
    return iterate


def collision_update_piece(
    convected_fields,
    discrete_abscissa_xaxis,
    discrete_abscissa_yaxis,
    discrete_abscissa_zaxis,
    particle_concentration,
    mean_drift_velocity,
    kinetic_thermal_level,
    energy_flux_components,
    collision_frequency,
    obstacle_indicators,
):
    diff_x = discrete_abscissa_xaxis - mean_drift_velocity[0]
    diff_y = discrete_abscissa_yaxis - mean_drift_velocity[1]
    diff_z = discrete_abscissa_zaxis - mean_drift_velocity[2]
    quadratic_deviation = diff_x * diff_x + diff_y * diff_y + diff_z * diff_z
    prefactor_amplitude = particle_concentration * kinetic_thermal_level ** (-1.5)
    local_gaussian_population = prefactor_amplitude * jnp.exp(
        -0.5 * quadratic_deviation / kinetic_thermal_level
    )
    skewed_correction_multiplier = (1.0 - momentum_thermal_ratio) / (
        5.0 * particle_concentration * kinetic_thermal_level * kinetic_thermal_level
    )
    projected_energy_flux = (
        diff_x * energy_flux_components[0]
        + diff_y * energy_flux_components[1]
        + diff_z * energy_flux_components[2]
    )
    goal_population = local_gaussian_population * (
        1.0
        + skewed_correction_multiplier
        * projected_energy_flux
        * (quadratic_deviation / kinetic_thermal_level - 5.0)
    )
    wall_state = particle_concentration * jnp.exp(
        -0.5
        * (
            discrete_abscissa_xaxis * discrete_abscissa_xaxis
            + discrete_abscissa_yaxis * discrete_abscissa_yaxis
            + discrete_abscissa_zaxis * discrete_abscissa_zaxis
        )
    )
    relaxed = convected_fields + collision_frequency * (goal_population - convected_fields)
    return jnp.where(obstacle_indicators > 0, wall_state, relaxed)


def per_device(distribution, rate_class, boundary_obstacle_indicator):
    vel_count, row_count, col_count = distribution.shape
    index = lax.axis_index("vel") * vel_count + jnp.arange(vel_count, dtype=jnp.int32)
    discrete_abscissa_xaxis, discrete_abscissa_yaxis, discrete_abscissa_zaxis = velocity_table(
        index
    )
    weights = moment_weights(
        discrete_abscissa_xaxis, discrete_abscissa_yaxis, discrete_abscissa_zaxis
    )
    column_x = discrete_abscissa_xaxis[:, None, None]
    column_y = discrete_abscissa_yaxis[:, None, None]
    column_z = discrete_abscissa_zaxis[:, None, None]
    courant_x = marching_step_length * column_x
    courant_y = marching_step_length * column_y
    reference_collision_freq = 0.5 * jnp.exp2(rate_class.astype(jnp.float32))
    field = distribution
    latest_conserved_fields = jnp.zeros((5, row_count, col_count), jnp.float32)
    for step_index in range(ITERS):
        convected_fields = transport(field, courant_x, courant_y)
        partial_value = jnp.dot(
            weights,
            convected_fields.reshape(vel_count, row_count * col_count),
            precision=lax.Precision.HIGHEST,
            preferred_element_type=jnp.float32,
        )
        moments = lax.psum(partial_value, "vel")
        source = conserved(moments)
        energy_flux_components = heat_flux(moments)
        source = source.reshape(5, row_count, col_count)
        energy_flux_components = energy_flux_components.reshape(3, row_count, col_count)
        latest_conserved_fields = diffuse(source)
        particle_concentration = latest_conserved_fields[0]
        mean_drift_velocity = latest_conserved_fields[1:4] / particle_concentration
        kinetic_thermal_level = (
            2.0 * latest_conserved_fields[4] / particle_concentration
            - (
                mean_drift_velocity[0] * mean_drift_velocity[0]
                + mean_drift_velocity[1] * mean_drift_velocity[1]
                + mean_drift_velocity[2] * mean_drift_velocity[2]
            )
        ) / 3.0
        collision_frequency = 1.0 - jnp.exp(
            -marching_step_length
            * reference_collision_freq
            * particle_concentration
            * kinetic_thermal_level ** (1.0 - shear_power_law_index)
        )
        field = collision_update_piece(
            convected_fields,
            column_x,
            column_y,
            column_z,
            particle_concentration,
            mean_drift_velocity,
            kinetic_thermal_level,
            energy_flux_components,
            collision_frequency,
            boundary_obstacle_indicator,
        )
    return (field, latest_conserved_fields)


def solution(mesh):
    placed = (P("vel", "space", None), P("space", None), P("space", None))
    return jax.shard_map(
        per_device,
        mesh=mesh,
        in_specs=placed,
        out_specs=(P("vel", "space", None), P(None, "space", None)),
        check_vma=False,
    )
```

profile of v0, /device:TPU:0, one launch (start us, length us, event | category | flops | bytes accessed | tf_op | source)
XLA Modules:
  0.0 239.6 jit_solution(17886712523408883976)
XLA Ops:
  0.6 4.2 %fusion.177 = (f32[1024,1,128]{2,1,0:T(1,128)S(1)}, f32[1024,1,128]{2,1,0:T(1,128)S(1)}) fusion(f32[1024,8,128]{2,1,0:T(8,128)} %param.3), kind=kLoop, calls=%fused_computation.291 | loop fusion | bytes 2097152 | tf_op jit(solution)/shard_map/slice | solution.py:23
  4.8 0.6 collective-permute-start.1
  6.1 5.4 %copy.27 = f32[1024,8,128]{0,2,1:T(8,128)} copy(f32[1024,8,128]{2,1,0:T(8,128)} %param.3) | data formatting | bytes 8388608 | tf_op args[0]
  11.4 1.1 fusion.176
  12.6 8.7 %fusion.175 = (f32[1024,8,127]{0,2,1:T(8,128)}, f32[1024,8,127]{0,2,1:T(8,128)}) fusion(f32[1024,8,128]{0,2,1:T(8,128)} %copy.27), kind=kLoop, calls=%fused_computation.289 | loop fusion | bytes 16646144 | tf_op jit(solution)/shard_map/jit(_roll_static)/slice | solution.py:118
  21.4 0.2 copy.25
  21.6 0.2 copy.20
  21.8 8.6 %fusion.47 = f32[1024,8,128]{0,2,1:T(8,128)S(1)} fusion(f32[1024,8,128]{0,2,1:T(8,128)} %copy.27, f32[1024,1,128]{0,2,1:T(8,128)S(1)} %copy.25, f32[1024,1,128]{0,2,1:T(8,128)S(1)} %copy.20, f32[1024,8,127]{0,2,1:T(8,128)} %get-tuple-element.17, f32[1024,8,1]{0,2,1:T(1,128)S(1)} %get-tuple-element.19, f32[1024,8,1]{0,2,1:T(1,128)S(1)} %get-tuple-element.18, ...), kind=kLoop, calls=%fused_computation.62 | loop fusion | flops 16777216 | bytes 17836032 | tf_op jit(solution)/shard_map/sub | solution.py:126
  30.4 2.0 copy-done.2
  32.4 3.6 %fusion.58 = f32[13,1024]{1,0:T(8,128)S(1)} fusion(f32[1024,1024]{0,1:T(8,128)S(1)} %bitcast.95, f32[13,1024]{1,0:T(8,128)S(1)} %stack.16), kind=kOutput, calls=%fused_computation.78 | convolution fusion | flops 163591168 | bytes 4300800 | tf_op jit(solution)/shard_map/dot_general | solution.py:207
  36.0 78.6 %psum.14 = f32[13,1024]{1,0:T(8,128)S(1)} all-reduce(f32[13,1024]{1,0:T(8,128)S(1)} %fusion.58), channel_id=1, replica_groups=mesh['vel'=16,'space'=2] {'vel'}, use_global_device_ids=true, to_apply=%region_0.1 | all-reduce | flops 13312 | bytes 106496 | tf_op jit(solution)/shard_map/psum | solution.py:213
  114.8 0.5 collective-permute-start.3
  115.3 0.6 collective-permute-done.2
  115.9 0.2 collective-permute-done.3
  117.2 7.4 %fusion.11 = f32[1024,8,128]{0,2,1:T(8,128)S(1)} fusion(f32[1024,8,128]{0,2,1:T(8,128)} %copy-done.2, f32[8,128]{1,0:T(8,128)S(1)} %bitcast.117, f32[8,128]{1,0:T(8,128)S(1)} %bitcast.115, f32[8,128]{1,0:T(8,128)S(1)} %bitcast.114, f32[8,128]{1,0:T(8,128)S(1)} %fusion.113, f32[8,128]{1,0:T(8,128)S(1)} %bitcast.111, f32[8,128]{1,0:T(8,128)S(1)} %get-tuple-element.71, ...), kind=kLoop, calls=%fused_computation.23 | loop fusion | flops 28311552 | bytes 8451072 | tf_op jit(solution)/shard_map/jit(_where)/select_n | solution.py:185
  124.7 1.9 copy-done
  126.7 0.2 copy.34
  126.9 0.2 copy.36
  127.1 0.4 collective-permute-start.5
  127.5 0.2 collective-permute-start.4
  127.7 8.7 %fusion.172 = (f32[1024,8,127]{0,2,1:T(8,128)}, f32[1024,8,127]{0,2,1:T(8,128)}) fusion(f32[1024,8,128]{0,2,1:T(8,128)} %copy-done), kind=kLoop, calls=%fused_computation.286 | loop fusion | bytes 16646144 | tf_op jit(solution)/shard_map/jit(_roll_static)/slice | solution.py:118
  136.5 0.2 copy.37
  136.7 0.2 copy.35
  136.9 8.6 %fusion.40 = f32[1024,8,128]{0,2,1:T(8,128)S(1)} fusion(f32[1024,8,128]{0,2,1:T(8,128)} %copy-done, f32[1024,1,128]{0,2,1:T(8,128)S(1)} %copy.37, f32[1024,1,128]{0,2,1:T(8,128)S(1)} %copy.35, f32[1024,8,127]{0,2,1:T(8,128)} %get-tuple-element.11, f32[1024,8,1]{0,2,1:T(1,128)S(1)} %get-tuple-element.13, f32[1024,8,1]{0,2,1:T(1,128)S(1)} %get-tuple-element.12, ...), kind=kLoop, calls=%fused_computation.53 | loop fusion | flops 16777216 | bytes 17836032 | tf_op jit(solution)/shard_map/sub | solution.py:126
  145.5 2.0 copy-done.1
  147.5 3.6 %fusion.56 = f32[13,1024]{1,0:T(8,128)S(1)} fusion(f32[1024,1024]{0,1:T(8,128)S(1)} %bitcast.94, f32[13,1024]{1,0:T(8,128)S(1)} %stack.16), kind=kOutput, calls=%fused_computation.76 | convolution fusion | flops 163591168 | bytes 4300800 | tf_op jit(solution)/shard_map/dot_general | solution.py:207
  151.1 71.8 %psum.15 = f32[13,1024]{1,0:T(8,128)S(1)} all-reduce(f32[13,1024]{1,0:T(8,128)S(1)} %fusion.56), channel_id=1, replica_groups=mesh['vel'=16,'space'=2] {'vel'}, use_global_device_ids=true, to_apply=%region_1.2 | all-reduce | flops 13312 | bytes 106496 | tf_op jit(solution)/shard_map/psum | solution.py:213
  223.0 0.5 collective-permute-start.7
  223.6 0.6 collective-permute-done.6
  224.2 0.2 collective-permute-done.7
  225.5 8.8 %fusion.29 = f32[1024,8,128]{0,2,1:T(8,128)} fusion(f32[1024,8,128]{0,2,1:T(8,128)} %copy-done.1, f32[8,128]{1,0:T(8,128)S(1)} %bitcast.116, f32[8,128]{1,0:T(8,128)S(1)} %bitcast.113, f32[8,128]{1,0:T(8,128)S(1)} %bitcast.112, f32[8,128]{1,0:T(8,128)S(1)} %fusion.115, f32[8,128]{1,0:T(8,128)S(1)} %bitcast.110, f32[8,128]{1,0:T(8,128)S(1)} %get-tuple-element.68, ...), kind=kLoop, calls=%fused_computation.41 | loop fusion | flops 28311552 | bytes 8451072 | tf_op jit(solution)/shard_map/jit(_where)/select_n | solution.py:185
  234.3 5.4 %copy.38 = f32[1024,8,128]{2,1,0:T(8,128)} copy(f32[1024,8,128]{0,2,1:T(8,128)} %fusion.29) | data formatting | bytes 8388608
  (77 shorter events, 3.5 us)
Async XLA Ops:
  4.8 16.6 %collective-permute-start.1 = (f32[1024,1,128]{2,0,1:T(8,128)S(1)}, f32[1024,1,128]{2,0,1:T(8,128)S(1)}, u32[]{:S(2)}, u32[]{:S(2)}) collective-permute-start(f32[1024,1,128]{2,0,1:T(8,128)S(1)} %bitcast.97), channel_id=1, source_target_pairs={{1,0},{0,1},{3,2},{2,3},{5,4},{4,5},{7,6},{6,7},{9,8},{8,9},{11,10... | collective-permute-start | bytes 1572872 | tf_op jit(solution)/shard_map/ppermute | solution.py:26
  5.4 16.2 %collective-permute-start = (f32[1024,1,128]{2,0,1:T(8,128)S(1)}, f32[1024,1,128]{2,0,1:T(8,128)S(1)}, u32[]{:S(2)}, u32[]{:S(2)}) collective-permute-start(f32[1024,1,128]{2,0,1:T(8,128)S(1)} %bitcast.96), channel_id=1, source_target_pairs={{0,1},{1,0},{2,3},{3,2},{4,5},{5,4},{6,7},{7,6},{8,9},{9,8},{10,11... | collective-permute-start | bytes 1572872 | tf_op jit(solution)/shard_map/ppermute | solution.py:25
  6.1 5.4 %copy-start.5 = (s32[8,128]{1,0:T(8,128)S(1)}, s32[8,128]{1,0:T(8,128)}, u32[]{:S(2)}) copy-start(s32[8,128]{1,0:T(8,128)} %param.5) | copy-start | bytes 12292
  30.4 2.0 copy-start.2
  30.4 86.7 %copy-start.4 = (s32[8,128]{1,0:T(8,128)S(1)}, s32[8,128]{1,0:T(8,128)}, u32[]{:S(2)}) copy-start(s32[8,128]{1,0:T(8,128)} %param.4) | copy-start | bytes 12292
  114.7 1.2 collective-permute-start.2
  114.8 1.3 collective-permute-start.3
  124.6 2.0 copy-start
  127.1 9.3 %collective-permute-start.5 = (f32[1024,1,128]{2,0,1:T(8,128)S(1)}, f32[1024,1,128]{2,0,1:T(8,128)S(1)}, u32[]{:S(2)}, u32[]{:S(2)}) collective-permute-start(f32[1024,1,128]{2,0,1:T(8,128)S(1)} %copy.36), channel_id=1, source_target_pairs={{1,0},{0,1},{3,2},{2,3},{5,4},{4,5},{7,6},{6,7},{9,8},{8,9},{11,10... | collective-permute-start | bytes 1572872 | tf_op jit(solution)/shard_map/ppermute | solution.py:26
  127.5 9.1 %collective-permute-start.4 = (f32[1024,1,128]{2,0,1:T(8,128)S(1)}, f32[1024,1,128]{2,0,1:T(8,128)S(1)}, u32[]{:S(2)}, u32[]{:S(2)}) collective-permute-start(f32[1024,1,128]{2,0,1:T(8,128)S(1)} %copy.34), channel_id=1, source_target_pairs={{0,1},{1,0},{2,3},{3,2},{4,5},{5,4},{6,7},{7,6},{8,9},{9,8},{10,11... | collective-permute-start | bytes 1572872 | tf_op jit(solution)/shard_map/ppermute | solution.py:25
  145.5 2.0 copy-start.1
  222.9 1.2 collective-permute-start.6
  223.0 1.3 collective-permute-start.7
  225.4 8.9 %copy-start.3 = (f32[5,8,128]{2,1,0:T(8,128)}, f32[5,8,128]{2,1,0:T(8,128)S(1)}, u32[]{:S(2)}) copy-start(f32[5,8,128]{2,1,0:T(8,128)S(1)} %fusion.87) | copy-start | bytes 61444
where the time goes:
time: 240 us
  blocking collectives  150 us (62%)
  local copies, waits for them, and re-layouts  42.1 us (18%)
  other arithmetic  35.1 us (15%)
  matrix products  7.12 us (3%)
    psum x2, blocking collectives, per_device(): moments = lax.psum(partial_value, 'vel')  150 us
    slice x4, local copies, waits for them, and re-layouts, transport(): from_right = jnp.roll(field, -1, 2)  18.6 us
    sub x2, other arithmetic, transport(): return field - term_x - term_y  17.2 us
    unnamed x18, local copies, waits for them, and re-layouts  16.7 us
    select_n x2, other arithmetic, collision_update_piece(): return jnp.where(obstacle_indicators > 0, wall_state, relaxed)  16.2 us
    dot_general x2, matrix products, per_device(): jnp.dot(weights, convected_fields.reshape(vel_count, row_count * col_coun...  7.12 us
  transfers between devices with their start and end apart: 8, of which 4 were waited for; matrix products, arithmetic and copies ran while one was open for 10% of the time, Pallas kernels for 0%

commit v1 on v0

--- a/solution.py
+++ b/solution.py
@@ -210,7 +210,11 @@
             precision=lax.Precision.HIGHEST,
             preferred_element_type=jnp.float32,
         )
-        moments = lax.psum(partial_value, "vel")
+        moments = partial_value
+        for hop in (1, 2, 4, 8):
+            moments = moments + lax.ppermute(
+                moments, "vel", [(dev, dev ^ hop) for dev in range(16)]
+            )
         source = conserved(moments)
         energy_flux_components = heat_flux(moments)
         source = source.reshape(5, row_count, col_count)

time: 240 us -> 119 us (0.50)
  blocking collectives: 150 us -> 0 us
  waiting for transfers between devices: 1.54 us -> 21.4 us
  starting transfers between devices: 2.35 us -> 20.9 us
  other arithmetic: 35.1 us -> 30.2 us
  local copies, waits for them, and re-layouts: 42.1 us -> 38.1 us
    psum x2 -> x0, blocking collectives: 150 us -> none  [per_device(): moments = lax.psum(partial_value, 'vel')]
    ppermute x0 -> x8, waiting for transfers between devices: none -> 19.9 us  [per_device(): lax.ppermute(moments, 'vel', [(dev, dev ^ hop) for dev in range(16)])]
    ppermute x0 -> x8, starting transfers between devices: none -> 18.6 us  [per_device(): lax.ppermute(moments, 'vel', [(dev, dev ^ hop) for dev in range(16)])]
    select_n x2, other arithmetic: 16.2 us -> 11 us  [collision_update_piece(): return jnp.where(obstacle_indicators > 0, wall_state, relaxed)]
    unnamed x18 -> x14, local copies, waits for them, and re-layouts: 16.7 us -> 12.7 us
  transfers between devices with their start and end apart: 8 -> 16, of which waited for: 4 -> 12; matrix products, arithmetic and copies ran while one was open for 10% -> 21% of each run, Pallas kernels for 0% -> 0%
where the time goes in v1:
time: 119 us
  local copies, waits for them, and re-layouts  38.1 us (32%)
  other arithmetic  30.2 us (25%)
  waiting for transfers between devices  21.4 us (18%)
  starting transfers between devices  20.9 us (18%)
  matrix products  7.13 us (6%)
    ppermute x8, waiting for transfers between devices, per_device(): lax.ppermute(moments, 'vel', [(dev, dev ^ hop) for dev in range(16)])  19.9 us
    slice x4, local copies, waits for them, and re-layouts, transport(): from_right = jnp.roll(field, -1, 2)  18.6 us
    ppermute x8, starting transfers between devices, per_device(): lax.ppermute(moments, 'vel', [(dev, dev ^ hop) for dev in range(16)])  18.6 us
    sub x2, other arithmetic, transport(): return field - term_x - term_y  17.4 us
    unnamed x14, local copies, waits for them, and re-layouts  12.7 us
    select_n x2, other arithmetic, collision_update_piece(): return jnp.where(obstacle_indicators > 0, wall_state, relaxed)  11 us
    dot_general x2, matrix products, per_device(): jnp.dot(weights, convected_fields.reshape(vel_count, row_count * col_coun...  7.13 us
    slice x3, local copies, waits for them, and re-layouts, with_halo(): last = lax.slice_in_dim(value, length - width, length, axis=dim)  4.45 us
  transfers between devices with their start and end apart: 16, of which 12 were waited for; matrix products, arithmetic and copies ran while one was open for 21% of the time, Pallas kernels for 0%

profile of v1, /device:TPU:0, one launch (start us, length us, event | category | flops | bytes accessed | tf_op | source)
XLA Modules:
  0.0 118.8 jit_solution(4816543170673697770)
XLA Ops:
  0.6 4.2 %fusion.177 = (f32[1024,1,128]{2,1,0:T(1,128)S(1)}, f32[1024,1,128]{2,1,0:T(1,128)S(1)}) fusion(f32[1024,8,128]{2,1,0:T(8,128)} %param.3), kind=kLoop, calls=%fused_computation.291 | loop fusion | bytes 2097152 | tf_op jit(solution)/shard_map/slice | solution.py:23
  4.8 0.6 collective-permute-start.1
  6.0 5.4 %copy.27 = f32[1024,8,128]{0,2,1:T(8,128)} copy(f32[1024,8,128]{2,1,0:T(8,128)} %param.3) | data formatting | bytes 8388608 | tf_op args[0]
  11.4 1.1 fusion.176
  12.6 8.7 %fusion.175 = (f32[1024,8,127]{0,2,1:T(8,128)}, f32[1024,8,127]{0,2,1:T(8,128)}) fusion(f32[1024,8,128]{0,2,1:T(8,128)} %copy.27), kind=kLoop, calls=%fused_computation.289 | loop fusion | bytes 16646144 | tf_op jit(solution)/shard_map/jit(_roll_static)/slice | solution.py:118
  21.8 8.6 %fusion.47 = f32[1024,8,128]{0,2,1:T(8,128)S(1)} fusion(f32[1024,8,128]{0,2,1:T(8,128)} %copy.27, f32[1024,1,128]{0,2,1:T(8,128)S(1)} %copy.25, f32[1024,1,128]{0,2,1:T(8,128)S(1)} %copy.20, f32[1024,8,127]{0,2,1:T(8,128)} %get-tuple-element.17, f32[1024,8,1]{0,2,1:T(1,128)S(1)} %get-tuple-element.19, f32[1024,8,1]{0,2,1:T(1,128)S(1)} %get-tuple-element.18, ...), kind=kLoop, calls=%fused_computation.62 | loop fusion | flops 16777216 | bytes 17836032 | tf_op jit(solution)/shard_map/sub | solution.py:126
  30.4 3.6 %fusion.58 = f32[13,1024]{1,0:T(8,128)S(1)} fusion(f32[1024,1024]{0,1:T(8,128)S(1)} %bitcast.95, f32[13,1024]{1,0:T(8,128)S(1)} %stack.16), kind=kOutput, calls=%fused_computation.78 | convolution fusion | flops 163591168 | bytes 4300800 | tf_op jit(solution)/shard_map/dot_general | solution.py:207
  34.0 2.9 %collective-permute-start.2 = (f32[13,1024]{1,0:T(8,128)S(1)}, f32[13,1024]{1,0:T(8,128)S(1)}, u32[]{:S(2)}, u32[]{:S(2)}) collective-permute-start(f32[13,1024]{1,0:T(8,128)S(1)} %fusion.58), channel_id=1, source_target_pairs={{0,2},{2,0},{4,6},{6,4},{8,10},{10,8},{12,14},{14,12},{16,18},{18,... | collective-permute-start | bytes 159752 | tf_op jit(solution)/shard_map/ppermute | solution.py:215
  36.9 2.3 %collective-permute-done.2 = f32[13,1024]{1,0:T(8,128)S(1)} collective-permute-done((f32[13,1024]{1,0:T(8,128)S(1)}, f32[13,1024]{1,0:T(8,128)S(1)}, u32[]{:S(2)}, u32[]{:S(2)}) %collective-permute-start.2) | collective-permute-done | bytes 53280 | tf_op jit(solution)/shard_map/ppermute | solution.py:215
  39.3 2.0 %collective-permute-start.3 = (f32[13,1024]{1,0:T(8,128)S(1)}, f32[13,1024]{1,0:T(8,128)S(1)}, u32[]{:S(2)}, u32[]{:S(2)}) collective-permute-start(f32[13,1024]{1,0:T(8,128)S(1)} %add.950), channel_id=1, source_target_pairs={{0,4},{2,6},{4,0},{6,2},{8,12},{10,14},{12,8},{14,10},{16,20},{18,... | collective-permute-start | bytes 159752 | tf_op jit(solution)/shard_map/ppermute | solution.py:215
  41.3 2.3 %collective-permute-done.3 = f32[13,1024]{1,0:T(8,128)S(1)} collective-permute-done((f32[13,1024]{1,0:T(8,128)S(1)}, f32[13,1024]{1,0:T(8,128)S(1)}, u32[]{:S(2)}, u32[]{:S(2)}) %collective-permute-start.3) | collective-permute-done | bytes 53280 | tf_op jit(solution)/shard_map/ppermute | solution.py:215
  43.6 2.1 %collective-permute-start.4 = (f32[13,1024]{1,0:T(8,128)S(1)}, f32[13,1024]{1,0:T(8,128)S(1)}, u32[]{:S(2)}, u32[]{:S(2)}) collective-permute-start(f32[13,1024]{1,0:T(8,128)S(1)} %add.951), channel_id=1, source_target_pairs={{0,8},{2,10},{4,12},{6,14},{8,0},{10,2},{12,4},{14,6},{16,24},{18,... | collective-permute-start | bytes 159752 | tf_op jit(solution)/shard_map/ppermute | solution.py:215
  45.7 2.2 %collective-permute-done.4 = f32[13,1024]{1,0:T(8,128)S(1)} collective-permute-done((f32[13,1024]{1,0:T(8,128)S(1)}, f32[13,1024]{1,0:T(8,128)S(1)}, u32[]{:S(2)}, u32[]{:S(2)}) %collective-permute-start.4) | collective-permute-done | bytes 53280 | tf_op jit(solution)/shard_map/ppermute | solution.py:215
  47.9 3.7 %collective-permute-start.5 = (f32[13,1024]{1,0:T(8,128)S(1)}, f32[13,1024]{1,0:T(8,128)S(1)}, u32[]{:S(2)}, u32[]{:S(2)}) collective-permute-start(f32[13,1024]{1,0:T(8,128)S(1)} %add.952), channel_id=1, source_target_pairs={{0,16},{2,18},{4,20},{6,22},{8,24},{10,26},{12,28},{14,30},{16,0},... | collective-permute-start | bytes 159752 | tf_op jit(solution)/shard_map/ppermute | solution.py:215
  51.7 2.2 %collective-permute-done.5 = f32[13,1024]{1,0:T(8,128)S(1)} collective-permute-done((f32[13,1024]{1,0:T(8,128)S(1)}, f32[13,1024]{1,0:T(8,128)S(1)}, u32[]{:S(2)}, u32[]{:S(2)}) %collective-permute-start.5) | collective-permute-done | bytes 53280 | tf_op jit(solution)/shard_map/ppermute | solution.py:215
  54.6 0.6 collective-permute-done.6
  56.5 4.6 %fusion.11 = f32[1024,8,128]{0,2,1:T(8,128)S(1)} fusion(f32[1024,8,128]{0,2,1:T(8,128)S(1)} %fusion.47, f32[8,128]{1,0:T(8,128)S(1)} %bitcast.117, f32[8,128]{1,0:T(8,128)S(1)} %bitcast.115, f32[8,128]{1,0:T(8,128)S(1)} %bitcast.114, f32[8,128]{1,0:T(8,128)S(1)} %fusion.113, f32[8,128]{1,0:T(8,128)S(1)} %bitcast.111, f32[8,128]{1,0:T(8,128)S(1)} %get-tuple-element.71, ...), kind=kLoop, calls=%fused_computation.23 | loop fusion | flops 28311552 | bytes 8451072 | tf_op jit(solution)/shard_map/jit(_where)/select_n | solution.py:185
  61.2 1.9 %copy-done = f32[1024,8,128]{0,2,1:T(8,128)} copy-done((f32[1024,8,128]{0,2,1:T(8,128)}, f32[1024,8,128]{0,2,1:T(8,128)S(1)}, u32[]{:S(2)}) %copy-start) | copy-done | bytes 4194328
  64.2 8.7 %fusion.172 = (f32[1024,8,127]{0,2,1:T(8,128)}, f32[1024,8,127]{0,2,1:T(8,128)}) fusion(f32[1024,8,128]{0,2,1:T(8,128)} %copy-done), kind=kLoop, calls=%fused_computation.286 | loop fusion | bytes 16646144 | tf_op jit(solution)/shard_map/jit(_roll_static)/slice | solution.py:118
  73.4 8.8 %fusion.40 = f32[1024,8,128]{0,2,1:T(8,128)S(1)} fusion(f32[1024,8,128]{0,2,1:T(8,128)} %copy-done, f32[1024,1,128]{0,2,1:T(8,128)S(1)} %copy.37, f32[1024,1,128]{0,2,1:T(8,128)S(1)} %copy.35, f32[1024,8,127]{0,2,1:T(8,128)} %get-tuple-element.11, f32[1024,8,1]{0,2,1:T(1,128)S(1)} %get-tuple-element.13, f32[1024,8,1]{0,2,1:T(1,128)S(1)} %get-tuple-element.12, ...), kind=kLoop, calls=%fused_computation.53 | loop fusion | flops 16777216 | bytes 17836032 | tf_op jit(solution)/shard_map/sub | solution.py:126
  82.2 3.6 %fusion.56 = f32[13,1024]{1,0:T(8,128)S(1)} fusion(f32[1024,1024]{0,1:T(8,128)S(1)} %bitcast.94, f32[13,1024]{1,0:T(8,128)S(1)} %stack.16), kind=kOutput, calls=%fused_computation.76 | convolution fusion | flops 163591168 | bytes 4300800 | tf_op jit(solution)/shard_map/dot_general | solution.py:207
  85.8 1.5 %collective-permute-start.10 = (f32[13,1024]{1,0:T(8,128)S(1)}, f32[13,1024]{1,0:T(8,128)S(1)}, u32[]{:S(2)}, u32[]{:S(2)}) collective-permute-start(f32[13,1024]{1,0:T(8,128)S(1)} %fusion.56), channel_id=1, source_target_pairs={{0,2},{2,0},{4,6},{6,4},{8,10},{10,8},{12,14},{14,12},{16,18},{18,... | collective-permute-start | bytes 159752 | tf_op jit(solution)/shard_map/ppermute | solution.py:215
  87.3 2.9 %collective-permute-done.10 = f32[13,1024]{1,0:T(8,128)S(1)} collective-permute-done((f32[13,1024]{1,0:T(8,128)S(1)}, f32[13,1024]{1,0:T(8,128)S(1)}, u32[]{:S(2)}, u32[]{:S(2)}) %collective-permute-start.10) | collective-permute-done | bytes 53280 | tf_op jit(solution)/shard_map/ppermute | solution.py:215
  90.1 1.6 %collective-permute-start.11 = (f32[13,1024]{1,0:T(8,128)S(1)}, f32[13,1024]{1,0:T(8,128)S(1)}, u32[]{:S(2)}, u32[]{:S(2)}) collective-permute-start(f32[13,1024]{1,0:T(8,128)S(1)} %add.995), channel_id=1, source_target_pairs={{0,4},{2,6},{4,0},{6,2},{8,12},{10,14},{12,8},{14,10},{16,20},{18,... | collective-permute-start | bytes 159752 | tf_op jit(solution)/shard_map/ppermute | solution.py:215
  91.7 2.7 %collective-permute-done.11 = f32[13,1024]{1,0:T(8,128)S(1)} collective-permute-done((f32[13,1024]{1,0:T(8,128)S(1)}, f32[13,1024]{1,0:T(8,128)S(1)}, u32[]{:S(2)}, u32[]{:S(2)}) %collective-permute-start.11) | collective-permute-done | bytes 53280 | tf_op jit(solution)/shard_map/ppermute | solution.py:215
  94.5 1.4 %collective-permute-start.12 = (f32[13,1024]{1,0:T(8,128)S(1)}, f32[13,1024]{1,0:T(8,128)S(1)}, u32[]{:S(2)}, u32[]{:S(2)}) collective-permute-start(f32[13,1024]{1,0:T(8,128)S(1)} %add.996), channel_id=1, source_target_pairs={{0,8},{2,10},{4,12},{6,14},{8,0},{10,2},{12,4},{14,6},{16,24},{18,... | collective-permute-start | bytes 159752 | tf_op jit(solution)/shard_map/ppermute | solution.py:215
  95.9 3.0 %collective-permute-done.12 = f32[13,1024]{1,0:T(8,128)S(1)} collective-permute-done((f32[13,1024]{1,0:T(8,128)S(1)}, f32[13,1024]{1,0:T(8,128)S(1)}, u32[]{:S(2)}, u32[]{:S(2)}) %collective-permute-start.12) | collective-permute-done | bytes 53280 | tf_op jit(solution)/shard_map/ppermute | solution.py:215
  98.8 3.4 %collective-permute-start.13 = (f32[13,1024]{1,0:T(8,128)S(1)}, f32[13,1024]{1,0:T(8,128)S(1)}, u32[]{:S(2)}, u32[]{:S(2)}) collective-permute-start(f32[13,1024]{1,0:T(8,128)S(1)} %add.997), channel_id=1, source_target_pairs={{0,16},{2,18},{4,20},{6,22},{8,24},{10,26},{12,28},{14,30},{16,0},... | collective-permute-start | bytes 159752 | tf_op jit(solution)/shard_map/ppermute | solution.py:215
  102.2 2.2 %collective-permute-done.13 = f32[13,1024]{1,0:T(8,128)S(1)} collective-permute-done((f32[13,1024]{1,0:T(8,128)S(1)}, f32[13,1024]{1,0:T(8,128)S(1)}, u32[]{:S(2)}, u32[]{:S(2)}) %collective-permute-start.13) | collective-permute-done | bytes 53280 | tf_op jit(solution)/shard_map/ppermute | solution.py:215
  105.2 0.6 collective-permute-done.14
  107.1 6.4 %fusion.29 = f32[1024,8,128]{0,2,1:T(8,128)} fusion(f32[1024,8,128]{0,2,1:T(8,128)S(1)} %fusion.40, f32[8,128]{1,0:T(8,128)S(1)} %bitcast.116, f32[8,128]{1,0:T(8,128)S(1)} %bitcast.113, f32[8,128]{1,0:T(8,128)S(1)} %bitcast.112, f32[8,128]{1,0:T(8,128)S(1)} %fusion.115, f32[8,128]{1,0:T(8,128)S(1)} %bitcast.110, f32[8,128]{1,0:T(8,128)S(1)} %get-tuple-element.68, ...), kind=kLoop, calls=%fused_computation.41 | loop fusion | flops 28311552 | bytes 8451072 | tf_op jit(solution)/shard_map/jit(_where)/select_n | solution.py:185
  113.5 5.4 %copy.38 = f32[1024,8,128]{2,1,0:T(8,128)} copy(f32[1024,8,128]{0,2,1:T(8,128)} %fusion.29) | data formatting | bytes 8388608
  (95 shorter events, 6.6 us)
Async XLA Ops:
  4.8 16.5 %collective-permute-start.1 = (f32[1024,1,128]{2,0,1:T(8,128)S(1)}, f32[1024,1,128]{2,0,1:T(8,128)S(1)}, u32[]{:S(2)}, u32[]{:S(2)}) collective-permute-start(f32[1024,1,128]{2,0,1:T(8,128)S(1)} %bitcast.97), channel_id=1, source_target_pairs={{1,0},{0,1},{3,2},{2,3},{5,4},{4,5},{7,6},{6,7},{9,8},{8,9},{11,10... | collective-permute-start | bytes 1572872 | tf_op jit(solution)/shard_map/ppermute | solution.py:26
  5.4 16.2 %collective-permute-start = (f32[1024,1,128]{2,0,1:T(8,128)S(1)}, f32[1024,1,128]{2,0,1:T(8,128)S(1)}, u32[]{:S(2)}, u32[]{:S(2)}) collective-permute-start(f32[1024,1,128]{2,0,1:T(8,128)S(1)} %bitcast.96), channel_id=1, source_target_pairs={{0,1},{1,0},{2,3},{3,2},{4,5},{5,4},{6,7},{7,6},{8,9},{9,8},{10,11... | collective-permute-start | bytes 1572872 | tf_op jit(solution)/shard_map/ppermute | solution.py:25
  30.4 15.3 %copy-start.3 = (s32[8,128]{1,0:T(8,128)S(1)}, s32[8,128]{1,0:T(8,128)}, u32[]{:S(2)}) copy-start(s32[8,128]{1,0:T(8,128)} %param.5) | copy-start | bytes 12292
  30.4 26.1 %copy-start.2 = (s32[8,128]{1,0:T(8,128)S(1)}, s32[8,128]{1,0:T(8,128)}, u32[]{:S(2)}) copy-start(s32[8,128]{1,0:T(8,128)} %param.4) | copy-start | bytes 12292
  34.0 5.3 %collective-permute-start.2 = (f32[13,1024]{1,0:T(8,128)S(1)}, f32[13,1024]{1,0:T(8,128)S(1)}, u32[]{:S(2)}, u32[]{:S(2)}) collective-permute-start(f32[13,1024]{1,0:T(8,128)S(1)} %fusion.58), channel_id=1, source_target_pairs={{0,2},{2,0},{4,6},{6,4},{8,10},{10,8},{12,14},{14,12},{16,18},{18,... | collective-permute-start | bytes 159752 | tf_op jit(solution)/shard_map/ppermute | solution.py:215
  39.3 4.3 %collective-permute-start.3 = (f32[13,1024]{1,0:T(8,128)S(1)}, f32[13,1024]{1,0:T(8,128)S(1)}, u32[]{:S(2)}, u32[]{:S(2)}) collective-permute-start(f32[13,1024]{1,0:T(8,128)S(1)} %add.950), channel_id=1, source_target_pairs={{0,4},{2,6},{4,0},{6,2},{8,12},{10,14},{12,8},{14,10},{16,20},{18,... | collective-permute-start | bytes 159752 | tf_op jit(solution)/shard_map/ppermute | solution.py:215
  43.6 4.3 %collective-permute-start.4 = (f32[13,1024]{1,0:T(8,128)S(1)}, f32[13,1024]{1,0:T(8,128)S(1)}, u32[]{:S(2)}, u32[]{:S(2)}) collective-permute-start(f32[13,1024]{1,0:T(8,128)S(1)} %add.951), channel_id=1, source_target_pairs={{0,8},{2,10},{4,12},{6,14},{8,0},{10,2},{12,4},{14,6},{16,24},{18,... | collective-permute-start | bytes 159752 | tf_op jit(solution)/shard_map/ppermute | solution.py:215
  47.9 5.9 %collective-permute-start.5 = (f32[13,1024]{1,0:T(8,128)S(1)}, f32[13,1024]{1,0:T(8,128)S(1)}, u32[]{:S(2)}, u32[]{:S(2)}) collective-permute-start(f32[13,1024]{1,0:T(8,128)S(1)} %add.952), channel_id=1, source_target_pairs={{0,16},{2,18},{4,20},{6,22},{8,24},{10,26},{12,28},{14,30},{16,0},... | collective-permute-start | bytes 159752 | tf_op jit(solution)/shard_map/ppermute | solution.py:215
  54.0 1.2 %collective-permute-start.6 = (f32[5,4,128]{2,1,0:T(4,128)S(1)}, f32[5,4,128]{2,1,0:T(4,128)S(1)}, u32[]{:S(2)}, u32[]{:S(2)}) collective-permute-start(f32[5,4,128]{2,1,0:T(4,128)S(1)} %get-tuple-element.64), channel_id=1, source_target_pairs={{0,1},{1,0},{2,3},{3,2},{4,5},{5,4},{6,7},{7,6},{8,9},{9,8},{10,11... | collective-permute-start | bytes 30728 | tf_op jit(solution)/shard_map/ppermute | solution.py:25
  54.1 1.3 %collective-permute-start.7 = (f32[5,4,128]{2,1,0:T(4,128)S(1)}, f32[5,4,128]{2,1,0:T(4,128)S(1)}, u32[]{:S(2)}, u32[]{:S(2)}) collective-permute-start(f32[5,4,128]{2,1,0:T(4,128)S(1)} %get-tuple-element.65), channel_id=1, source_target_pairs={{1,0},{0,1},{3,2},{2,3},{5,4},{4,5},{7,6},{6,7},{9,8},{8,9},{11,10... | collective-permute-start | bytes 30728 | tf_op jit(solution)/shard_map/ppermute | solution.py:26
  61.2 2.0 %copy-start = (f32[1024,8,128]{0,2,1:T(8,128)}, f32[1024,8,128]{0,2,1:T(8,128)S(1)}, u32[]{:S(2)}) copy-start(f32[1024,8,128]{0,2,1:T(8,128)S(1)} %fusion.11) | copy-start | bytes 12582916
  63.7 9.3 %collective-permute-start.9 = (f32[1024,1,128]{2,0,1:T(8,128)S(1)}, f32[1024,1,128]{2,0,1:T(8,128)S(1)}, u32[]{:S(2)}, u32[]{:S(2)}) collective-permute-start(f32[1024,1,128]{2,0,1:T(8,128)S(1)} %copy.36), channel_id=1, source_target_pairs={{1,0},{0,1},{3,2},{2,3},{5,4},{4,5},{7,6},{6,7},{9,8},{8,9},{11,10... | collective-permute-start | bytes 1572872 | tf_op jit(solution)/shard_map/ppermute | solution.py:26
  64.1 9.1 %collective-permute-start.8 = (f32[1024,1,128]{2,0,1:T(8,128)S(1)}, f32[1024,1,128]{2,0,1:T(8,128)S(1)}, u32[]{:S(2)}, u32[]{:S(2)}) collective-permute-start(f32[1024,1,128]{2,0,1:T(8,128)S(1)} %copy.34), channel_id=1, source_target_pairs={{0,1},{1,0},{2,3},{3,2},{4,5},{5,4},{6,7},{7,6},{8,9},{9,8},{10,11... | collective-permute-start | bytes 1572872 | tf_op jit(solution)/shard_map/ppermute | solution.py:25
  85.8 4.4 %collective-permute-start.10 = (f32[13,1024]{1,0:T(8,128)S(1)}, f32[13,1024]{1,0:T(8,128)S(1)}, u32[]{:S(2)}, u32[]{:S(2)}) collective-permute-start(f32[13,1024]{1,0:T(8,128)S(1)} %fusion.56), channel_id=1, source_target_pairs={{0,2},{2,0},{4,6},{6,4},{8,10},{10,8},{12,14},{14,12},{16,18},{18,... | collective-permute-start | bytes 159752 | tf_op jit(solution)/shard_map/ppermute | solution.py:215
  90.1 4.3 %collective-permute-start.11 = (f32[13,1024]{1,0:T(8,128)S(1)}, f32[13,1024]{1,0:T(8,128)S(1)}, u32[]{:S(2)}, u32[]{:S(2)}) collective-permute-start(f32[13,1024]{1,0:T(8,128)S(1)} %add.995), channel_id=1, source_target_pairs={{0,4},{2,6},{4,0},{6,2},{8,12},{10,14},{12,8},{14,10},{16,20},{18,... | collective-permute-start | bytes 159752 | tf_op jit(solution)/shard_map/ppermute | solution.py:215
  94.5 4.3 %collective-permute-start.12 = (f32[13,1024]{1,0:T(8,128)S(1)}, f32[13,1024]{1,0:T(8,128)S(1)}, u32[]{:S(2)}, u32[]{:S(2)}) collective-permute-start(f32[13,1024]{1,0:T(8,128)S(1)} %add.996), channel_id=1, source_target_pairs={{0,8},{2,10},{4,12},{6,14},{8,0},{10,2},{12,4},{14,6},{16,24},{18,... | collective-permute-start | bytes 159752 | tf_op jit(solution)/shard_map/ppermute | solution.py:215
  98.8 5.6 %collective-permute-start.13 = (f32[13,1024]{1,0:T(8,128)S(1)}, f32[13,1024]{1,0:T(8,128)S(1)}, u32[]{:S(2)}, u32[]{:S(2)}) collective-permute-start(f32[13,1024]{1,0:T(8,128)S(1)} %add.997), channel_id=1, source_target_pairs={{0,16},{2,18},{4,20},{6,22},{8,24},{10,26},{12,28},{14,30},{16,0},... | collective-permute-start | bytes 159752 | tf_op jit(solution)/shard_map/ppermute | solution.py:215
  104.6 1.2 %collective-permute-start.14 = (f32[5,4,128]{2,1,0:T(4,128)S(1)}, f32[5,4,128]{2,1,0:T(4,128)S(1)}, u32[]{:S(2)}, u32[]{:S(2)}) collective-permute-start(f32[5,4,128]{2,1,0:T(4,128)S(1)} %get-tuple-element.62), channel_id=1, source_target_pairs={{0,1},{1,0},{2,3},{3,2},{4,5},{5,4},{6,7},{7,6},{8,9},{9,8},{10,11... | collective-permute-start | bytes 30728 | tf_op jit(solution)/shard_map/ppermute | solution.py:25
  104.7 1.3 %collective-permute-start.15 = (f32[5,4,128]{2,1,0:T(4,128)S(1)}, f32[5,4,128]{2,1,0:T(4,128)S(1)}, u32[]{:S(2)}, u32[]{:S(2)}) collective-permute-start(f32[5,4,128]{2,1,0:T(4,128)S(1)} %get-tuple-element.63), channel_id=1, source_target_pairs={{1,0},{0,1},{3,2},{2,3},{5,4},{4,5},{7,6},{6,7},{9,8},{8,9},{11,10... | collective-permute-start | bytes 30728 | tf_op jit(solution)/shard_map/ppermute | solution.py:26
  107.0 6.5 %copy-start.1 = (f32[5,8,128]{2,1,0:T(8,128)}, f32[5,8,128]{2,1,0:T(8,128)S(1)}, u32[]{:S(2)}) copy-start(f32[5,8,128]{2,1,0:T(8,128)S(1)} %fusion.87) | copy-start | bytes 61444
